TPU v7x, 128 devices: a whole 4x4x4 slice. The times are simulated.
128 devices in a mesh: blk: 32 (over x, z, y_hi), quarter: 4 (over y_lo, core).
Axes of the slice: x: 4, y: 4 (y_hi: 2, y_lo: 2; y = y_hi * 2 + y_lo), z: 4, core: 2. Of those that a mesh axis runs over, the one named last changes fastest.
Arguments:
- bints: bfloat16 [256, 512, 1280], P('blk', None, 'quarter'), may hold values from -2.5 to 2.5
- occ_energy: float32 [256], replicated, may hold values from -2 to -0.5
- vir_energy: float32 [512], replicated, may hold values from 0.2 to 3
Outputs:
- gamma: float32 [256, 512, 1280], P(('blk', 'quarter'))
- vvdens: float32 [512, 512], P(('blk', 'quarter'))
All inputs are finite; a program needn't handle non-finite values.
Results may differ from a plain program's by a relative error of at most 0.0016.
Values may be sent and summed in bfloat16 or wider, within the bound.
A program may use at most 128 MiB of HBM per device.

v0:
```python
import jax
import jax.numpy as jnp
from jax import lax
from jax.sharding import PartitionSpec as P

V = 512
CYCLE = 3


def shifted(shard, axis, by):
    devices = lax.axis_size(axis)
    return lax.ppermute(shard, axis, [(i, (i + by) % devices) for i in range(devices)])


def per_device(bints, occ_energy, vir_energy):
    local = lax.all_to_all(bints, "quarter", split_axis=0, concat_axis=2, tiled=True)
    quarters = lax.axis_size("quarter")
    block_count = lax.axis_size("blk")
    block_id = lax.axis_index("blk")
    quarter_id = lax.axis_index("quarter")
    occ_rows = local.shape[0]
    own_group = block_id * quarters + quarter_id
    own_energy = lax.dynamic_slice_in_dim(occ_energy, own_group * occ_rows, occ_rows)
    density = jnp.zeros(local.shape, jnp.float32)
    vv_part = jnp.zeros((V, V), jnp.float32)
    partner_block = local
    for step in range(CYCLE):
        if step > 0:
            partner_block = shifted(partner_block, "blk", 1)
        partner = (block_id - step) % block_count * quarters + quarter_id
        other_energy = lax.dynamic_slice_in_dim(occ_energy, partner * occ_rows, occ_rows)
        pairint = jnp.einsum(
            "iap,jbp->ijab", local, partner_block, preferred_element_type=jnp.float32
        )
        denom = (
            vir_energy[None, None, :, None]
            + vir_energy[None, None, None, :]
            - own_energy[:, None, None, None]
            - other_energy[None, :, None, None]
        )
        amp = pairint / denom
        amp_b = amp.astype(jnp.bfloat16)
        tilde = (2.0 * amp - jnp.swapaxes(amp, 2, 3)).astype(jnp.bfloat16)
        density = density + jnp.einsum(
            "ijab,jbp->iap", tilde, partner_block, preferred_element_type=jnp.float32
        )
        vv_part = vv_part + jnp.einsum(
            "ijac,ijbc->ab", amp_b, tilde, preferred_element_type=jnp.float32
        )
    row_count = V // (block_count * quarters)
    summed = lax.psum(vv_part, ("blk", "quarter"))
    rows_out = lax.dynamic_slice_in_dim(summed, own_group * row_count, row_count, 0)
    return (density, rows_out / PAIRS_SCALE(occ_rows, block_count, quarters))


def PAIRS_SCALE(occ_rows, block_count, quarters):
    return float(occ_rows * block_count * quarters * CYCLE * occ_rows)


def solution(mesh):
    return jax.shard_map(
        per_device,
        mesh=mesh,
        in_specs=(P("blk", None, "quarter"), P(), P()),
        out_specs=(P(("blk", "quarter"), None, None), P(("blk", "quarter"), None)),
        check_vma=False,
    )
```

profile of v0, /device:TPU:1, one launch (start us, length us, event | category | flops | bytes accessed | tf_op | source)
XLA Modules:
  0.0 359.4 jit_solution(8892862195207607736)
XLA Ops:
  7.2 0.0 all-reduce.2.cloned.1.call-start
  7.2 35.3 %all_to_all.18 = bf16[8,512,320]{1,2,0:T(8,128)(2,1)S(1)} all-to-all(bf16[8,512,320]{1,2,0:T(8,128)(2,1)} %param.3), channel_id=1, replica_groups=mesh['blk'=32,'quarter'=4] {'quarter'}, dimensions={0} | all-to-all | bytes 5242880 | tf_op jit(solution)/shard_map/all_to_all | solution.py:16
  42.5 0.0 copy-start
  42.5 0.2 copy.21
  42.6 1.3 copy-done
  44.0 0.0 copy-start.9
  44.0 0.0 copy-start.8
  44.0 2.6 copy.25
  46.5 3.0 collective-permute-start
  49.6 62.2 %collective-permute-done = bf16[2,512,1280]{2,1,0:T(8,128)(2,1)} collective-permute-done((bf16[2,512,1280]{2,1,0:T(8,128)(2,1)}, bf16[2,512,1280]{2,1,0:T(8,128)(2,1)}, u32[]{:S(2)}, u32[]{:S(2)}) %collective-permute-start) | collective-permute-done | bytes 2621472 | tf_op jit(solution)/shard_map/ppermute | solution.py:12
  111.7 0.0 collective-permute-start.1
  111.7 0.0 copy-done.9
  111.8 0.0 copy-start.1
  111.8 0.1 fusion.54
  111.8 0.0 copy-done.8
  111.8 0.1 broadcast_add_fusion
  112.0 1.7 broadcast_subtract_fusion
  113.6 0.3 copy-done.1
  113.9 4.5 %fusion.13 = f32[2,512,2,512,1]{3,1,4,2,0:T(8,128)} fusion(bf16[4,2,512,320]{2,3,1,0:T(8,128)(2,1)S(1)} %bitcast.95), kind=kOutput, calls=%fused_computation.21 | convolution fusion | flops 2684354560 | bytes 6815744 | tf_op jit(solution)/shard_map/iap,jbp->ijab/dot_general | solution.py:32
  118.4 5.2 %copy.22 = f32[2,512,2,512]{1,3,2,0:T(8,128)} copy(f32[2,512,2,512]{3,1,2,0:T(8,128)} %bitcast.89) | data formatting | bytes 8388608 | tf_op jit(solution)/shard_map/iap,jbp->ijab/dot_general | solution.py:32
  123.6 6.2 %fusion.11 = f32[2,512,2,512]{3,1,2,0:T(8,128)} fusion(bf16[2,512,1280,1]{1,2,0,3:T(8,128)(2,1)S(1)} %bitcast.91, bf16[2,512,1280]{2,1,0:T(8,128)(2,1)} %collective-permute-done), kind=kOutput, calls=%fused_computation.19 | convolution fusion | flops 2684354560 | bytes 9437184 | tf_op jit(solution)/shard_map/iap,jbp->ijab/dot_general | solution.py:32
  129.8 5.3 %copy.27 = f32[2,512,2,512]{1,3,2,0:T(8,128)} copy(f32[2,512,2,512]{3,1,2,0:T(8,128)} %fusion.11) | data formatting | bytes 8388608 | tf_op jit(solution)/shard_map/iap,jbp->ijab/dot_general | solution.py:32
  135.1 39.5 %collective-permute-done.1 = bf16[2,512,1280]{2,1,0:T(8,128)(2,1)} collective-permute-done((bf16[2,512,1280]{2,1,0:T(8,128)(2,1)}, bf16[2,512,1280]{2,1,0:T(8,128)(2,1)}, u32[]{:S(2)}, u32[]{:S(2)}) %collective-permute-start.1) | collective-permute-done | bytes 2621472 | tf_op jit(solution)/shard_map/ppermute | solution.py:12
  174.6 6.1 %fusion.7 = f32[2,512,2,512]{3,1,2,0:T(8,128)} fusion(bf16[2,512,1280,1]{1,2,0,3:T(8,128)(2,1)S(1)} %bitcast.92, bf16[2,512,1280]{2,1,0:T(8,128)(2,1)} %collective-permute-done.1), kind=kOutput, calls=%fused_computation.15 | convolution fusion | flops 2684354560 | bytes 9437184 | tf_op jit(solution)/shard_map/iap,jbp->ijab/dot_general | solution.py:32
  180.7 5.2 %copy.30 = f32[2,512,2,512]{1,3,2,0:T(8,128)} copy(f32[2,512,2,512]{3,1,2,0:T(8,128)} %fusion.7) | data formatting | bytes 8388608 | tf_op jit(solution)/shard_map/iap,jbp->ijab/dot_general | solution.py:32
  185.9 12.9 %fusion.52 = (bf16[2,2,512,512]{3,2,0,1:T(8,128)(2,1)S(1)}, bf16[2,2,512,512]{3,2,0,1:T(8,128)(2,1)S(1)}, bf16[2,2,512,512]{3,2,0,1:T(8,128)(2,1)S(1)}, bf16[2,2...) fusion(f32[2]{0:T(128)S(1)} %get-tuple-element.12, ...), kind=kLoop, calls=%fused_computation.42 | loop fusion | flops 22020096 | bytes 39845912 | tf_op jit(solution)/shard_map/convert_element_type | solution.py:42
  198.8 0.0 copy-start.6
  198.8 0.0 copy-start.4
  198.8 0.0 copy-start.2
  198.9 0.0 copy-start.7
  198.9 4.6 %fusion.25 = f32[512,512]{1,0:T(8,128)S(1)} fusion(bf16[2,2,512,512]{3,2,0,1:T(8,128)(2,1)S(1)} %get-tuple-element.10, bf16[2,2,512,512]{3,2,0,1:T(8,128)(2,1)} %get-tuple-element.11), kind=kOutput, calls=%fused_computation.33 | convolution fusion | flops 1073741824 | bytes 5242880 | tf_op jit(solution)/shard_map/ijac,ijbc->ab/dot_general | solution.py:47
  203.4 0.0 copy-done.6
  203.5 0.0 copy-done.4
  203.5 0.0 copy-done.7
  203.5 1.3 fusion.45
  204.8 0.0 copy-done.2
  204.8 2.3 fusion.40
  207.1 0.0 all-reduce.2.cloned.1.call-update
  207.1 0.0 copy-start.5
  207.1 4.6 %fusion.55 = f32[2,512,1280,1]{2,1,0,3:T(8,128)S(1)} fusion(bf16[2,2,512,512]{3,2,0,1:T(8,128)(2,1)} %copy-done.6, bf16[2,512,1280,1]{1,2,3,0:T(8,128)(2,1)S(1)} %bitcast.93), kind=kOutput, calls=%fused_computation.46 | convolution fusion | flops 2684354560 | bytes 9961472 | tf_op jit(solution)/shard_map/ijab,jbp->iap/dot_general | solution.py:44
  211.7 0.0 copy-done.5
  211.7 0.0 copy-start.3
  211.8 4.8 %fusion.9 = f32[2,512,1280,1]{2,1,0,3:T(8,128)S(1)} fusion(bf16[2,2,512,512]{3,2,0,1:T(8,128)(2,1)S(1)} %copy-done.5, bf16[2,512,1280]{2,1,0:T(8,128)(2,1)} %collective-permute-done), kind=kOutput, calls=%fused_computation.17 | convolution fusion | flops 2684354560 | bytes 9961472 | tf_op jit(solution)/shard_map/ijab,jbp->iap/dot_general | solution.py:44
  216.5 0.0 copy-done.3
  216.5 6.3 %bitcast_add_fusion = f32[2,512,1280]{2,1,0:T(8,128)} fusion(f32[2,512,1280,1]{2,1,0,3:T(8,128)S(1)} %fusion.9, f32[2,512,1280,1]{2,1,0,3:T(8,128)S(1)} %fusion.55, bf16[2,2,512,512]{3,2,0,1:T(8,128)(2,1)S(1)} %copy-done.3, bf16[2,512,1280]{2,1,0:T(8,128)(2,1)} %collective-permute-done.1), kind=kOutput, calls=%fused_computation.6 | convolution fusion | flops 2686976000 | bytes 20447232 | tf_op jit(solution)/shard_map/ijab,jbp->iap/dot_general | solution.py:44
  222.9 128.3 %all-reduce.2.cloned.1.call-done = f32[512,512]{1,0:T(8,128)} async-done(((f32[512,512]{1,0:T(8,128)}), f32[512,512]{1,0:T(8,128)}) %all-reduce.2.cloned.1.call-update) | async-done | bytes 1048592 | tf_op jit(solution)/shard_map/psum | solution.py:51
  351.2 1.3 dynamic-slice_multiply_fusion
Async XLA Ops:
  7.2 344.1 %all-reduce.2.cloned.1.call-start = ((), (), s32[]{:S(2)}) async-start(), calls=%async_computation.1 | async-start | bytes 2097152 | tf_op jit(solution)/shard_map/psum | solution.py:51
  42.5 1.5 copy-start
  44.0 67.8 %copy-start.9 = (f32[256]{0:T(256)S(1)}, f32[256]{0:T(256)}, u32[]{:S(2)}) copy-start(f32[256]{0:T(256)} %param.4) | copy-start | bytes 3076
  44.0 67.9 %copy-start.8 = (f32[512]{0:T(512)S(1)}, f32[512]{0:T(512)}, u32[]{:S(2)}) copy-start(f32[512]{0:T(512)} %param.5) | copy-start | bytes 6148
  46.5 65.2 %collective-permute-start = (bf16[2,512,1280]{2,1,0:T(8,128)(2,1)}, bf16[2,512,1280]{2,1,0:T(8,128)(2,1)}, u32[]{:S(2)}, u32[]{:S(2)}) collective-permute-start(bf16[2,512,1280]{2,1,0:T(8,128)(2,1)} %copy.25), channel_id=1, source_target_pairs={{0,4},{4,8},{8,12},{12,16},{16,20},{20,24},{24,28},{28,32},{32,36}... | collective-permute-start | bytes 7864328 | tf_op jit(solution)/shard_map/ppermute | solution.py:12
  111.7 62.8 %collective-permute-start.1 = (bf16[2,512,1280]{2,1,0:T(8,128)(2,1)}, bf16[2,512,1280]{2,1,0:T(8,128)(2,1)}, u32[]{:S(2)}, u32[]{:S(2)}) collective-permute-start(bf16[2,512,1280]{2,1,0:T(8,128)(2,1)} %collective-permute-done), channel_id=1, source_target_pairs={{0,4},{4,8},{8,12},{12,16},{16,20},{20,24},{24,28},{28,32},{32,36}... | collective-permute-start | bytes 7864328 | tf_op jit(solution)/shard_map/ppermute | solution.py:12
  111.8 2.2 copy-start.1
  198.8 4.6 %copy-start.6 = (bf16[2,2,512,512]{3,2,0,1:T(8,128)(2,1)}, bf16[2,2,512,512]{3,2,0,1:T(8,128)(2,1)S(1)}, u32[]{:S(2)}) copy-start(bf16[2,2,512,512]{3,2,0,1:T(8,128)(2,1)S(1)} %get-tuple-element.10) | copy-start | bytes 6291460
  198.8 4.6 %copy-start.4 = (bf16[2,2,512,512]{3,2,0,1:T(8,128)(2,1)}, bf16[2,2,512,512]{3,2,0,1:T(8,128)(2,1)S(1)}, u32[]{:S(2)}) copy-start(bf16[2,2,512,512]{3,2,0,1:T(8,128)(2,1)S(1)} %get-tuple-element.8) | copy-start | bytes 6291460
  198.8 5.9 %copy-start.2 = (bf16[2,2,512,512]{3,2,0,1:T(8,128)(2,1)}, bf16[2,2,512,512]{3,2,0,1:T(8,128)(2,1)S(1)}, u32[]{:S(2)}) copy-start(bf16[2,2,512,512]{3,2,0,1:T(8,128)(2,1)S(1)} %get-tuple-element.3) | copy-start | bytes 6291460
  198.9 4.6 %copy-start.7 = (bf16[2,2,512,512]{3,2,0,1:T(8,128)(2,1)S(1)}, bf16[2,2,512,512]{3,2,0,1:T(8,128)(2,1)}, u32[]{:S(2)}) copy-start(bf16[2,2,512,512]{3,2,0,1:T(8,128)(2,1)} %get-tuple-element.9) | copy-start | bytes 6291460
  207.1 4.7 %copy-start.5 = (bf16[2,2,512,512]{3,2,0,1:T(8,128)(2,1)S(1)}, bf16[2,2,512,512]{3,2,0,1:T(8,128)(2,1)}, u32[]{:S(2)}) copy-start(bf16[2,2,512,512]{3,2,0,1:T(8,128)(2,1)} %copy-done.4) | copy-start | bytes 6291460
  211.7 4.8 %copy-start.3 = (bf16[2,2,512,512]{3,2,0,1:T(8,128)(2,1)S(1)}, bf16[2,2,512,512]{3,2,0,1:T(8,128)(2,1)}, u32[]{:S(2)}) copy-start(bf16[2,2,512,512]{3,2,0,1:T(8,128)(2,1)} %copy-done.2) | copy-start | bytes 6291460
Sparse Core Ops, SparseCore 0:
  207.2 143.9 all-reduce.1
where the time goes:
time: 360 us; the launch traced here: 359 us
  waiting for transfers between devices  230 us (64%)
  matrix products  40.6 us (11%)
  blocking collectives  35.3 us (10%)
  local copies, waits for them, and re-layouts  20.2 us (6%)
  other arithmetic  16 us (4%)
  between operations  14.2 us (4%)
    psum x1, waiting for transfers between devices, per_device(): summed = lax.psum(vv_part, ('blk', 'quarter'))  128 us
    ppermute x2, waiting for transfers between devices, shifted(): lax.ppermute(shard, axis, [(i, (i + by) % devices) for i in range(devices)])  102 us
    all_to_all x1, blocking collectives, per_device(): lax.all_to_all(bints, 'quarter', split_axis=0, concat_axis=2, tiled=True)  35.3 us
    dot_general x3, matrix products, per_device(): jnp.einsum('iap,jbp->ijab', local, partner_block, preferred_element_type=...  16.8 us
    dot_general x3, local copies, waits for them, and re-layouts, per_device(): jnp.einsum('iap,jbp->ijab', local, partner_block, preferred_element_type=...  15.8 us
    dot_general x3, matrix products, per_device(): jnp.einsum('ijab,jbp->iap', tilde, partner_block, preferred_element_type=...  15.7 us
    convert_element_type x1, other arithmetic, per_device(): amp_b = amp.astype(jnp.bfloat16)  12.9 us
    dot_general x3, matrix products, per_device(): jnp.einsum('ijac,ijbc->ab', amp_b, tilde, preferred_element_type=jnp.floa...  8.13 us
  transfers between devices with their start and end apart: 3, of which 3 were waited for; matrix products, arithmetic and copies ran while one was open for 11% of the time, Pallas kernels for 0%

commit v1 on v0

v1 whole, which is shorter than its diff:
```python
import functools

import jax
import jax.numpy as jnp
from jax import lax
from jax.experimental import pallas as pl
from jax.experimental.pallas import tpu as pltpu
from jax.sharding import PartitionSpec as P

CYCLE = 3
RING = 4
MESH = pl.DeviceIdType.MESH
NT = (((1,), (1,)), ((), ()))
X, Y, Z = 0, 1, 2


def kernel(
    blocks,
    scale,
    x_ref,
    occ_ref,
    vir_ref,
    gamma_ref,
    vv_ref,
    held,
    raw,
    own_t,
    acc,
    vv,
    amp,
    amp_b,
    tilde,
    vir_col,
    halves,
    half_in,
    by_y,
    by_z,
    by_x,
    local_sem,
    send_sem,
    recv_sem,
    raw_sem,
    out_sem,
    vv_send,
    vv_recv,
):
    piece = x_ref.shape[1]
    b, q = lax.axis_index("blk"), lax.axis_index("quarter")
    col, h, l, k = b // 2, lax.rem(b, 2), q // 2, lax.rem(q, 2)
    cx, cz = col // RING, lax.rem(col, RING)
    near = [q, 2 * l + 1 - k, 2 * (1 - l) + k, 2 * (1 - l) + 1 - k]
    ahead, behind = lax.rem(b + 2, blocks), lax.rem(b + blocks - 2, blocks)
    across = 2 * col + 1 - h

    def along_z(step):
        return 2 * (cx * RING + lax.rem(cz + step, RING)) + h

    def along_x(step):
        return 2 * (lax.rem(cx + step, RING) * RING + cz) + h

    barrier = pltpu.get_barrier_semaphore()
    peers = [(b, near[d]) for d in (1, 2, 3)] + [(across, near[d]) for d in range(4)] + [(ahead, q), (behind, q)]
    peers += [(along_z(s), q) for s in (1, 2, 3)] + [(along_x(s), q) for s in (1, 2, 3)]
    for peer in peers:
        pl.semaphore_signal(barrier, inc=1, device_id=peer, device_id_type=MESH)

    def slot(which, j, p):
        return held.at[which * 2 + j, pl.ds(pl.multiple_of(p * piece, piece), piece), :]

    sends = {0: 0, 1: 0}

    def send(side, src, dst, sem, device):
        n = sends[side]
        copy = pltpu.make_async_remote_copy(
            src_ref=src, dst_ref=dst, send_sem=send_sem.at[n], recv_sem=sem, device_id=device, device_id_type=MESH
        )
        copy.start()
        sends[side] = n + 1

    def to_slot(side, src, which, j, p, device):
        send(side, src, slot(which, j, p), recv_sem.at[which, j, p], device)

    def arrived(dst, sem):
        pltpu.make_async_remote_copy(
            src_ref=dst, dst_ref=dst, send_sem=send_sem.at[0], recv_sem=sem, device_id=(b, near[1]), device_id_type=MESH
        ).wait_recv()

    def slot_arrived(which, j, p):
        arrived(slot(which, j, p), recv_sem.at[which, j, p])

    def mine(r, j):
        return x_ref.at[2 * r + j]

    own_copies = [pltpu.make_async_copy(mine(q, j), slot(X, j, q), local_sem.at[j]) for j in range(2)]
    for copy in own_copies:
        copy.start()
    pl.semaphore_wait(barrier, len(peers))

    @pl.when(h == 0)
    def _():
        for j in range(2):
            for d in (1, 2, 3):
                to_slot(0, mine(near[d], j), X, j, q, (b, near[d]))
            to_slot(0, mine(q, j), Y, j, q, (ahead, q))
            for d in (2, 3):
                to_slot(0, mine(near[d], j), Y, j, q, (across, near[d]))
        for j in range(2):
            for d in (0, 1):
                to_slot(0, mine(near[d], j), Y, j, q, (across, near[d]))

    @pl.when(h == 1)
    def _():
        for j in range(2):
            for d in (1, 2, 3):
                to_slot(1, mine(near[d], j), X, j, q, (b, near[d]))
            to_slot(1, mine(q, j), Z, j, q, (ahead, q))
            for d in (1, 2, 3):
                send(1, mine(near[d], j), raw.at[j, d - 1], raw_sem.at[j, d - 1], (ahead, q))

    acc[...] = jnp.zeros_like(acc)
    vv[...] = jnp.zeros_like(vv)
    vir_col[...] = jnp.transpose(jnp.broadcast_to(vir_ref[...], (128, vir_ref.shape[1])))

    def own_piece(j, d):
        slot_arrived(X, j, near[d])

        @pl.when(h == 0)
        def _():
            to_slot(0, slot(X, j, near[d]), Y, j, near[d], (ahead, q))

    def passed_on(j, d):
        @pl.when(h == 1)
        def _():
            if d == 0:
                slot_arrived(Z, j, q)
                to_slot(1, slot(Z, j, q), Z, j, q, (across, q))
                return
            src = raw.at[j, d - 1]
            arrived(src, raw_sem.at[j, d - 1])
            to_slot(1, src, Z, j, q, (across, near[d]))
            if d == 1 or j == 0:
                to_slot(1, src, Z, j, q, (b, near[d]))

    def second_way():
        @pl.when(h == 1)
        def _():
            for d in (2, 3):
                to_slot(1, slot(X, 1, near[d]), Z, 1, near[d], (ahead, q))

    def last_piece(j):
        @pl.when(h == 0)
        def _():
            slot_arrived(Z, j, q)

        for d in (1, 2, 3):
            slot_arrived(Z, j, near[d])

    def turned(i):
        for n in range(held.shape[1] // 256):
            rows = pl.ds(n * 256, 256)
            own_t[i, :, rows] = jnp.transpose(held[2 * X + i, rows, :])

    def before(t):
        @pl.when(t == 1)
        def _():
            own_piece(1, 2)
            passed_on(0, 2)
            own_piece(1, 3)
            passed_on(0, 3)
            second_way()
            turned(1)

        @pl.when(t == 3)
        def _():
            passed_on(1, 0)

        @pl.when(t == 4)
        def _():
            passed_on(1, 1)
            for p in range(4):
                slot_arrived(Y, 0, p)

        @pl.when(t == 6)
        def _():
            passed_on(1, 2)
            last_piece(0)

        @pl.when(t == 8)
        def _():
            passed_on(1, 3)
            for p in range(4):
                slot_arrived(Y, 1, p)

        @pl.when(t == 10)
        def _():
            last_piece(1)

    for copy in own_copies:
        copy.wait()
    own_piece(0, 1)
    own_piece(1, 1)
    own_piece(0, 2)
    passed_on(0, 0)
    own_piece(0, 3)
    passed_on(0, 1)
    turned(0)

    size = vir_ref.shape[1]

    def pair(t, carry):
        before(t)
        turn, i = t // 2, lax.rem(t, 2)
        which = jnp.where(turn < 2, X, Y + lax.rem(turn, 2))
        j = jnp.where(turn < 2, turn, (turn - 2) // 2)
        back = jnp.where(turn < 2, 0, jnp.where(which == Y, 2 - h, 1 + h))
        partner = lax.rem(b - back + blocks, blocks)
        e_i = occ_ref[(b * 4 + q) * 2 + i]
        e_j = occ_ref[(partner * 4 + q) * 2 + j]
        other = held.at[which * 2 + j]
        for n in range(size // 256):
            cols = pl.ds(n * 256, 256)
            pairint = jnp.dot(own_t[i], other[:, cols], preferred_element_type=jnp.float32)
            for m in range(2):
                lanes = pl.ds(n * 256 + m * 128, 128)
                denom = vir_col[...] + vir_ref[:, lanes] - e_i - e_j
                ratio = pairint[:, m * 128 : (m + 1) * 128] / denom
                amp[:, lanes] = ratio
                amp_b[:, lanes] = ratio.astype(jnp.bfloat16)
        for n in range(size // 128):
            rows = pl.ds(n * 128, 128)
            tilde[rows, :] = (2.0 * amp[rows, :] - jnp.transpose(amp[:, rows])).astype(jnp.bfloat16)
        vv[...] += lax.dot_general(amp_b[...], tilde[...], NT, preferred_element_type=jnp.float32)
        for n in range(held.shape[1] // 256):
            rows = pl.ds(n * 256, 256)
            acc[i, :, rows] += lax.dot_general(tilde[...], other[rows, :], NT, preferred_element_type=jnp.float32)
        return carry

    lax.fori_loop(0, 4 * CYCLE, pair, 0)

    out = pltpu.make_async_copy(acc, gamma_ref, out_sem)
    out.start()

    low = lax.broadcasted_iota(jnp.int32, (8, 256), 0) < 4
    for chip in range(size // 8):
        spot = (chip % RING) * RING * RING + ((chip // RING) % RING) * RING + chip // (RING * RING)
        rows = pl.ds(chip * 8, 8)
        left, right = vv[rows, 0:256], vv[rows, 256:512]
        halves[0, spot] = jnp.where(low, left, pltpu.roll(right, 4, 0))
        halves[1, spot] = jnp.where(low, pltpu.roll(left, 4, 0), right)

    swap = pltpu.make_async_remote_copy(
        src_ref=halves.at[1 - k], dst_ref=half_in, send_sem=vv_send.at[0], recv_sem=vv_recv.at[0],
        device_id=(b, near[1]), device_id_type=MESH,
    )
    swap.start()
    swap.wait()

    def stage(src, landing, first, me, devices):
        copies = [
            pltpu.make_async_remote_copy(
                src_ref=src.at[lax.rem(me + s, RING)], dst_ref=landing.at[s - 1],
                send_sem=vv_send.at[first + s - 1], recv_sem=vv_recv.at[first + s - 1],
                device_id=devices[s - 1], device_id_type=MESH,
            )
            for s in (1, 2, 3)
        ]
        for copy in copies:
            copy.start()
        for copy in copies:
            copy.wait()
        return src[me] + landing[0] + landing[1] + landing[2]

    here = 2 * h + l
    column = []
    for s in (1, 2, 3):
        there = lax.rem(here + s, RING)
        column.append((2 * col + there // 2, 2 * lax.rem(there, 2) + k))
    half_in[...] += halves[k]
    by_chip = half_in.reshape(RING, RING * RING, 8, 256)
    by_z_src = stage(by_chip, by_y, 1, here, column)
    halves[0, 0:16] = by_z_src
    by_row = halves.at[0, pl.ds(0, 16)].reshape(RING, RING, 8, 256)
    by_x_src = stage(by_row, by_z, 4, cz, [(along_z(s), q) for s in (1, 2, 3)])
    halves[1, 0:4] = by_x_src
    total = stage(halves.at[1, pl.ds(0, 4)], by_x, 7, cx, [(along_x(s), q) for s in (1, 2, 3)]) * scale
    vv_ref[:, 0:256] = total[0:4]
    vv_ref[:, 256:512] = total[4:8]

    for side in (0, 1):

        @pl.when(h == side)
        def _():
            for n in range(sends[side]):
                pltpu.make_async_remote_copy(
                    src_ref=x_ref.at[0], dst_ref=raw.at[0, 0], send_sem=send_sem.at[n], recv_sem=recv_sem.at[0, 0, 0],
                    device_id=(b, near[1]), device_id_type=MESH,
                ).wait_send()

    out.wait()


def per_device(blocks, quarters, bints, occ_energy, vir_energy):
    rows, size, piece = bints.shape
    naux = piece * quarters
    pair_rows = rows // quarters
    f32, bf16 = jnp.float32, jnp.bfloat16
    scale = 1.0 / float(pair_rows * blocks * quarters * CYCLE * pair_rows)
    dma = pltpu.SemaphoreType.DMA
    chips = size // 8
    return pl.pallas_call(
        functools.partial(kernel, blocks, scale),
        out_shape=(
            jax.ShapeDtypeStruct((pair_rows, size, naux), f32),
            jax.ShapeDtypeStruct((size // (blocks * quarters), size), f32),
        ),
        in_specs=[
            pl.BlockSpec(memory_space=pl.ANY),
            pl.BlockSpec(memory_space=pltpu.SMEM),
            pl.BlockSpec(memory_space=pltpu.VMEM),
        ],
        out_specs=(pl.BlockSpec(memory_space=pl.ANY), pl.BlockSpec(memory_space=pltpu.VMEM)),
        scratch_shapes=[
            pltpu.VMEM((3 * pair_rows, naux, size), bf16),
            pltpu.VMEM((pair_rows, 3, piece, size), bf16),
            pltpu.VMEM((pair_rows, size, naux), bf16),
            pltpu.VMEM((pair_rows, size, naux), f32),
            pltpu.VMEM((size, size), f32),
            pltpu.VMEM((size, size), f32),
            pltpu.VMEM((size, size), bf16),
            pltpu.VMEM((size, size), bf16),
            pltpu.VMEM((size, 128), f32),
            pltpu.VMEM((2, chips, 8, 256), f32),
            pltpu.VMEM((chips, 8, 256), f32),
            pltpu.VMEM((3, 16, 8, 256), f32),
            pltpu.VMEM((3, 4, 8, 256), f32),
            pltpu.VMEM((3, 8, 256), f32),
            dma((2,)),
            dma((40,)),
            dma((3, 2, 4)),
            dma((2, 3)),
            dma,
            dma((10,)),
            dma((10,)),
        ],
        compiler_params=pltpu.CompilerParams(
            collective_id=0, has_side_effects=True, vmem_limit_bytes=60 * 2**20
        ),
        name="pair_densities",
    )(jnp.swapaxes(bints, 1, 2), occ_energy, vir_energy.reshape(1, size))


def solution(mesh):
    return jax.shard_map(
        functools.partial(per_device, mesh.shape["blk"], mesh.shape["quarter"]),
        mesh=mesh,
        in_specs=(P("blk", None, "quarter"), P(), P()),
        out_specs=(P(("blk", "quarter"), None, None), P(("blk", "quarter"), None)),
        check_vma=False,
    )
```

time: 360 us -> 120 us (0.33)
  waiting for transfers between devices: 230 us -> 0 us
  Pallas kernels: 0 us -> 112 us
  matrix products: 40.6 us -> 0 us
  blocking collectives: 35.3 us -> 0 us
  other arithmetic: 16 us -> 0 us
  local copies, waits for them, and re-layouts: 20.2 us -> 5.79 us
  between operations: 14.2 us -> 0.65 us
    psum x1 -> x0, waiting for transfers between devices: 128 us -> none  [per_device(): summed = lax.psum(vv_part, ('blk', 'quarter'))]
    pallas_call x0 -> x1, Pallas kernels: none -> 112 us  [per_device(): pl.pallas_call(functools.partial(kernel, blocks, scale), out_shape=(jax.S...]
    ppermute x2 -> x0, waiting for transfers between devices: 102 us -> none  [shifted(): lax.ppermute(shard, axis, [(i, (i + by) % devices) for i in range(devices)])]
    dot_general x9 -> x0, matrix products: 40.6 us -> none  [the longest x3 16.8 us: per_device(): jnp.einsum('iap,jbp->ijab', local, partner_block, preferred_element_type=...]
    all_to_all x1 -> x0, blocking collectives: 35.3 us -> none  [per_device(): lax.all_to_all(bints, 'quarter', split_axis=0, concat_axis=2, tiled=True)]
    dot_general x3 -> x0, local copies, waits for them, and re-layouts: 15.8 us -> none  [per_device(): jnp.einsum('iap,jbp->ijab', local, partner_block, preferred_element_type=...]
    convert_element_type x1 -> x0, other arithmetic: 12.9 us -> none  [per_device(): amp_b = amp.astype(jnp.bfloat16)]
    unnamed x20 -> x4, local copies, waits for them, and re-layouts: 1.63 us -> 5.79 us
  transfers between devices with their start and end apart: 3 -> 0, of which waited for: 3 -> 0; matrix products, arithmetic and copies ran while one was open for 11% -> 0% of each run, Pallas kernels for 0% -> 0%
where the time goes in v1:
time: 120 us; the launch traced here: 118 us
  Pallas kernels  112 us (93%)
  local copies, waits for them, and re-layouts  5.79 us (5%)
    pallas_call x1, Pallas kernels, per_device(): pl.pallas_call(functools.partial(kernel, blocks, scale), out_shape=(jax.S...  112 us
    unnamed x4, local copies, waits for them, and re-layouts  5.79 us

profile of v1, /device:TPU:1, one launch (start us, length us, event | category | flops | bytes accessed | tf_op | source)
XLA Modules:
  0.0 118.3 jit_solution(5960664303919076281)
XLA Ops:
  0.6 111.9 %pair_densities.1 = (f32[2,512,1280]{2,1,0:T(8,128)}, f32[4,512]{1,0:T(4,128)}) custom-call(bf16[8,320,512]{2,1,0:T(8,128)(2,1)} %bitcast.2, f32[256]{0:T(256)} %occ_ref.1, f32[1,512]{1,0:T(1,128)} %bitcast.3), custom_call_target="tpu_custom_call" | custom-call | tf_op jit(solution)/shard_map/pair_densities/pallas_call | solution.py:310
  112.5 0.0 copy-start
  112.5 5.2 %copy.7 = f32[2,512,1280]{2,1,0:T(8,128)} copy(f32[2,512,1280]{2,1,0:T(8,128)} %get-tuple-element.4) | data formatting | bytes 10485760
  117.7 0.0 copy-done
  117.7 0.6 copy.8
Async XLA Ops:
  112.5 5.2 %copy-start = (f32[4,512]{1,0:T(4,128)S(1)}, f32[4,512]{1,0:T(4,128)}, u32[]{:S(2)}) copy-start(f32[4,512]{1,0:T(4,128)} %get-tuple-element.5) | copy-start | bytes 24580

commit v2 on v1

--- a/solution.py
+++ b/solution.py
@@ -20,12 +20,12 @@
     x_ref,
     occ_ref,
     vir_ref,
-    gamma_ref,
+    acc,
     vv_ref,
     held,
     raw,
+    relay,
     own_t,
-    acc,
     vv,
     amp,
     amp_b,
@@ -33,14 +33,16 @@
     vir_col,
     halves,
     half_in,
-    by_y,
-    by_z,
-    by_x,
+    first_in,
+    second,
+    second_in,
+    third,
+    third_in,
     local_sem,
     send_sem,
     recv_sem,
     raw_sem,
-    out_sem,
+    relay_sem,
     vv_send,
     vv_recv,
 ):
@@ -98,23 +100,30 @@
 
     @pl.when(h == 0)
     def _():
-        for j in range(2):
-            for d in (1, 2, 3):
-                to_slot(0, mine(near[d], j), X, j, q, (b, near[d]))
-            to_slot(0, mine(q, j), Y, j, q, (ahead, q))
-            for d in (2, 3):
-                to_slot(0, mine(near[d], j), Y, j, q, (across, near[d]))
+        for d in (1, 2, 3):
+            to_slot(0, mine(near[d], 0), X, 0, q, (b, near[d]))
+        to_slot(0, mine(near[1], 1), X, 1, q, (b, near[1]))
+        to_slot(0, mine(q, 0), Y, 0, q, (ahead, q))
+        for d in (2, 3):
+            to_slot(0, mine(near[d], 0), Y, 0, q, (across, near[d]))
+        for d in (2, 3):
+            to_slot(0, mine(near[d], 1), X, 1, q, (b, near[d]))
+        to_slot(0, mine(q, 1), Y, 1, q, (ahead, q))
+        for d in (2, 3):
+            to_slot(0, mine(near[d], 1), Y, 1, q, (across, near[d]))
         for j in range(2):
             for d in (0, 1):
                 to_slot(0, mine(near[d], j), Y, j, q, (across, near[d]))
 
     @pl.when(h == 1)
     def _():
+        send(1, mine(near[3], 1), relay.at[0], relay_sem.at[0], (across, near[3]))
+        for d in (1, 2, 3):
+            to_slot(1, mine(near[d], 0), X, 0, q, (b, near[d]))
+        to_slot(1, mine(near[1], 1), X, 1, q, (b, near[1]))
         for j in range(2):
-            for d in (1, 2, 3):
-                to_slot(1, mine(near[d], j), X, j, q, (b, near[d]))
             to_slot(1, mine(q, j), Z, j, q, (ahead, q))
-            for d in (1, 2, 3):
+            for d in (1, 2, 3)[: 3 - j]:
                 send(1, mine(near[d], j), raw.at[j, d - 1], raw_sem.at[j, d - 1], (ahead, q))
 
     acc[...] = jnp.zeros_like(acc)
@@ -133,7 +142,12 @@
         def _():
             if d == 0:
                 slot_arrived(Z, j, q)
+                if j == 1:
+                    send(1, slot(Z, j, q), relay.at[1], relay_sem.at[1], (across, near[2]))
+                    return
                 to_slot(1, slot(Z, j, q), Z, j, q, (across, q))
+                for own in (2, 3):
+                    to_slot(1, mine(near[own], 1), X, 1, q, (b, near[own]))
                 return
             src = raw.at[j, d - 1]
             arrived(src, raw_sem.at[j, d - 1])
@@ -147,6 +161,15 @@
             for d in (2, 3):
                 to_slot(1, slot(X, 1, near[d]), Z, 1, near[d], (ahead, q))
 
+    def relayed(n):
+        @pl.when(h == 0)
+        def _():
+            arrived(relay.at[n], relay_sem.at[n])
+            if n == 0:
+                to_slot(0, relay.at[n], Z, 1, near[3], (ahead, q))
+            else:
+                to_slot(0, relay.at[n], Z, 1, near[2], (b, near[2]))
+
     def last_piece(j):
         @pl.when(h == 0)
         def _():
@@ -163,20 +186,19 @@
     def before(t):
         @pl.when(t == 1)
         def _():
+            passed_on(0, 2)
             own_piece(1, 2)
-            passed_on(0, 2)
+            passed_on(0, 3)
             own_piece(1, 3)
-            passed_on(0, 3)
             second_way()
+            relayed(0)
+            passed_on(1, 0)
             turned(1)
 
-        @pl.when(t == 3)
-        def _():
-            passed_on(1, 0)
-
         @pl.when(t == 4)
         def _():
             passed_on(1, 1)
+            relayed(1)
             for p in range(4):
                 slot_arrived(Y, 0, p)
 
@@ -187,7 +209,6 @@
 
         @pl.when(t == 8)
         def _():
-            passed_on(1, 3)
             for p in range(4):
                 slot_arrived(Y, 1, p)
 
@@ -207,12 +228,25 @@
 
     size = vir_ref.shape[1]
 
+    pairs = 4 * CYCLE
+
+    def place(t):
+        turn = t // 2
+        which = jnp.where(turn < 2, X, Y + lax.rem(turn, 2))
+        j = jnp.where(turn < 2, turn, (turn - 2) // 2)
+        return lax.rem(t, 2), which, j
+
+    def to_gamma(t):
+        i, which, j = place(t)
+        other = held.at[which * 2 + j]
+        for n in range(held.shape[1] // 256):
+            rows = pl.ds(n * 256, 256)
+            acc[i, :, rows] += lax.dot_general(tilde[i], other[rows, :], NT, preferred_element_type=jnp.float32)
+
     def pair(t, carry):
         before(t)
-        turn, i = t // 2, lax.rem(t, 2)
-        which = jnp.where(turn < 2, X, Y + lax.rem(turn, 2))
-        j = jnp.where(turn < 2, turn, (turn - 2) // 2)
-        back = jnp.where(turn < 2, 0, jnp.where(which == Y, 2 - h, 1 + h))
+        i, which, j = place(t)
+        back = jnp.where(which == X, 0, jnp.where(which == Y, 2 - h, 1 + h))
         partner = lax.rem(b - back + blocks, blocks)
         e_i = occ_ref[(b * 4 + q) * 2 + i]
         e_j = occ_ref[(partner * 4 + q) * 2 + j]
@@ -228,34 +262,50 @@
                 amp_b[:, lanes] = ratio.astype(jnp.bfloat16)
         for n in range(size // 128):
             rows = pl.ds(n * 128, 128)
-            tilde[rows, :] = (2.0 * amp[rows, :] - jnp.transpose(amp[:, rows])).astype(jnp.bfloat16)
-        vv[...] += lax.dot_general(amp_b[...], tilde[...], NT, preferred_element_type=jnp.float32)
-        for n in range(held.shape[1] // 256):
-            rows = pl.ds(n * 256, 256)
-            acc[i, :, rows] += lax.dot_general(tilde[...], other[rows, :], NT, preferred_element_type=jnp.float32)
+            tilde[i, rows, :] = (2.0 * amp[rows, :] - jnp.transpose(amp[:, rows])).astype(jnp.bfloat16)
+        vv[...] += lax.dot_general(amp_b[...], tilde[i], NT, preferred_element_type=jnp.float32)
+
+        @pl.when(t < pairs - 2)
+        def _():
+            to_gamma(t)
+
         return carry
 
-    lax.fori_loop(0, 4 * CYCLE, pair, 0)
-
-    out = pltpu.make_async_copy(acc, gamma_ref, out_sem)
-    out.start()
+    lax.fori_loop(0, pairs, pair, 0)
 
     low = lax.broadcasted_iota(jnp.int32, (8, 256), 0) < 4
+    square = RING * RING
     for chip in range(size // 8):
-        spot = (chip % RING) * RING * RING + ((chip // RING) % RING) * RING + chip // (RING * RING)
+        spot = (chip % RING) * square + ((chip // RING) % RING) * RING + chip // square
         rows = pl.ds(chip * 8, 8)
         left, right = vv[rows, 0:256], vv[rows, 256:512]
-        halves[0, spot] = jnp.where(low, left, pltpu.roll(right, 4, 0))
-        halves[1, spot] = jnp.where(low, pltpu.roll(left, 4, 0), right)
+        for core, block in enumerate((jnp.where(low, left, pltpu.roll(right, 4, 0)), jnp.where(low, pltpu.roll(left, 4, 0), right))):
+            halves[core, 0, spot] = block[:, 0:128]
+            halves[core, 1, chip] = block[:, 128:256]
 
     swap = pltpu.make_async_remote_copy(
         src_ref=halves.at[1 - k], dst_ref=half_in, send_sem=vv_send.at[0], recv_sem=vv_recv.at[0],
         device_id=(b, near[1]), device_id_type=MESH,
     )
     swap.start()
+    to_gamma(pairs - 2)
+    to_gamma(pairs - 1)
     swap.wait()
-
-    def stage(src, landing, first, me, devices):
+    half_in[...] += halves[k]
+
+    here = 2 * h + l
+    column = []
+    for s in (1, 2, 3):
+        there = lax.rem(here + s, RING)
+        column.append((2 * col + there // 2, 2 * lax.rem(there, 2) + k))
+    rings = {
+        "y": (here, column),
+        "z": (cz, [(along_z(s), q) for s in (1, 2, 3)]),
+        "x": (cx, [(along_x(s), q) for s in (1, 2, 3)]),
+    }
+
+    def stage(src, landing, first, axis):
+        me, devices = rings[axis]
         copies = [
             pltpu.make_async_remote_copy(
                 src_ref=src.at[lax.rem(me + s, RING)], dst_ref=landing.at[s - 1],
@@ -266,25 +316,27 @@
         ]
         for copy in copies:
             copy.start()
-        for copy in copies:
-            copy.wait()
-        return src[me] + landing[0] + landing[1] + landing[2]
-
-    here = 2 * h + l
-    column = []
-    for s in (1, 2, 3):
-        there = lax.rem(here + s, RING)
-        column.append((2 * col + there // 2, 2 * lax.rem(there, 2) + k))
-    half_in[...] += halves[k]
-    by_chip = half_in.reshape(RING, RING * RING, 8, 256)
-    by_z_src = stage(by_chip, by_y, 1, here, column)
-    halves[0, 0:16] = by_z_src
-    by_row = halves.at[0, pl.ds(0, 16)].reshape(RING, RING, 8, 256)
-    by_x_src = stage(by_row, by_z, 4, cz, [(along_z(s), q) for s in (1, 2, 3)])
-    halves[1, 0:4] = by_x_src
-    total = stage(halves.at[1, pl.ds(0, 4)], by_x, 7, cx, [(along_x(s), q) for s in (1, 2, 3)]) * scale
-    vv_ref[:, 0:256] = total[0:4]
-    vv_ref[:, 256:512] = total[4:8]
+
+        def total():
+            for copy in copies:
+                copy.wait()
+            return src[me] + landing[0] + landing[1] + landing[2]
+
+        return total
+
+    orders = ("yzx", "xzy")
+    waits = [stage(half_in.at[n].reshape(RING, square, 8, 128), first_in.at[n], 1 + 3 * n, orders[n][0]) for n in range(2)]
+    for n in range(2):
+        second[n] = waits[n]()
+        waits[n] = stage(second.at[n].reshape(RING, RING, 8, 128), second_in.at[n], 7 + 3 * n, orders[n][1])
+    for n in range(2):
+        third[n] = waits[n]()
+        waits[n] = stage(third.at[n], third_in.at[n], 13 + 3 * n, orders[n][2])
+    for n in range(2):
+        total = waits[n]() * scale
+        lanes = pl.ds(n * 128, 128)
+        vv_ref[:, lanes] = total[0:4]
+        vv_ref[:, pl.ds(256 + n * 128, 128)] = total[4:8]
 
     for side in (0, 1):
 
@@ -295,8 +347,6 @@
                     src_ref=x_ref.at[0], dst_ref=raw.at[0, 0], send_sem=send_sem.at[n], recv_sem=recv_sem.at[0, 0, 0],
                     device_id=(b, near[1]), device_id_type=MESH,
                 ).wait_send()
-
-    out.wait()
 
 
 def per_device(blocks, quarters, bints, occ_energy, vir_energy):
@@ -314,36 +364,38 @@
             jax.ShapeDtypeStruct((size // (blocks * quarters), size), f32),
         ),
         in_specs=[
-            pl.BlockSpec(memory_space=pl.ANY),
+            pl.BlockSpec(memory_space=pltpu.HBM),
             pl.BlockSpec(memory_space=pltpu.SMEM),
             pl.BlockSpec(memory_space=pltpu.VMEM),
         ],
-        out_specs=(pl.BlockSpec(memory_space=pl.ANY), pl.BlockSpec(memory_space=pltpu.VMEM)),
+        out_specs=(pl.BlockSpec(memory_space=pltpu.VMEM), pl.BlockSpec(memory_space=pltpu.VMEM)),
         scratch_shapes=[
             pltpu.VMEM((3 * pair_rows, naux, size), bf16),
             pltpu.VMEM((pair_rows, 3, piece, size), bf16),
+            pltpu.VMEM((2, piece, size), bf16),
             pltpu.VMEM((pair_rows, size, naux), bf16),
-            pltpu.VMEM((pair_rows, size, naux), f32),
             pltpu.VMEM((size, size), f32),
             pltpu.VMEM((size, size), f32),
             pltpu.VMEM((size, size), bf16),
-            pltpu.VMEM((size, size), bf16),
+            pltpu.VMEM((pair_rows, size, size), bf16),
             pltpu.VMEM((size, 128), f32),
-            pltpu.VMEM((2, chips, 8, 256), f32),
-            pltpu.VMEM((chips, 8, 256), f32),
-            pltpu.VMEM((3, 16, 8, 256), f32),
-            pltpu.VMEM((3, 4, 8, 256), f32),
-            pltpu.VMEM((3, 8, 256), f32),
+            pltpu.VMEM((2, 2, chips, 8, 128), f32),
+            pltpu.VMEM((2, chips, 8, 128), f32),
+            pltpu.VMEM((2, 3, 16, 8, 128), f32),
+            pltpu.VMEM((2, 16, 8, 128), f32),
+            pltpu.VMEM((2, 3, 4, 8, 128), f32),
+            pltpu.VMEM((2, 4, 8, 128), f32),
+            pltpu.VMEM((2, 3, 8, 128), f32),
             dma((2,)),
             dma((40,)),
             dma((3, 2, 4)),
             dma((2, 3)),
-            dma,
-            dma((10,)),
-            dma((10,)),
+            dma((2,)),
+            dma((19,)),
+            dma((19,)),
         ],
         compiler_params=pltpu.CompilerParams(
-            collective_id=0, has_side_effects=True, vmem_limit_bytes=60 * 2**20
+            collective_id=0, has_side_effects=True, vmem_limit_bytes=40 * 2**20
         ),
         name="pair_densities",
     )(jnp.swapaxes(bints, 1, 2), occ_energy, vir_energy.reshape(1, size))

time: 120 us -> 101 us (0.84)
  Pallas kernels: 112 us -> 92.7 us
    pallas_call x1, Pallas kernels: 112 us -> 92.7 us  [per_device(): pl.pallas_call(functools.partial(kernel, blocks, scale), out_shape=(jax.S...]
    unnamed x4 -> x8, local copies, waits for them, and re-layouts: 5.79 us -> 6.05 us
where the time goes in v2:
time: 101 us; the launch traced here: 99.4 us
  Pallas kernels  92.7 us (92%)
  local copies, waits for them, and re-layouts  6.05 us (6%)
    pallas_call x1, Pallas kernels, per_device(): pl.pallas_call(functools.partial(kernel, blocks, scale), out_shape=(jax.S...  92.7 us
    unnamed x8, local copies, waits for them, and re-layouts  6.05 us

profile of v2, /device:TPU:1, one launch (start us, length us, event | category | flops | bytes accessed | tf_op | source)
XLA Modules:
  0.0 99.4 jit_solution(13209986517445307061)
XLA Ops:
  0.6 0.0 copy-start
  0.6 1.7 %copy-done = bf16[8,512,320]{1,2,0:T(8,128)(2,1)S(1)} copy-done((bf16[8,512,320]{1,2,0:T(8,128)(2,1)S(1)}, bf16[8,512,320]{1,2,0:T(8,128)(2,1)}, u32[]{:S(2)}) %copy-start) | copy-done | bytes 2621464
  2.4 0.0 copy-start.1
  2.4 0.7 copy-done.1
  3.1 0.0 copy-start.2
  3.1 0.7 copy-done.2
  3.7 92.7 %pair_densities.1 = (f32[2,512,1280]{2,1,0:T(8,128)S(1)}, f32[4,512]{1,0:T(4,128)S(1)}) custom-call(bf16[8,320,512]{2,1,0:T(8,128)(2,1)S(1)} %bitcast.2, f32[256]{0:T(256)S(1)} %copy-done.2, f32[1,512]{1,0:T(1,128)S(1)} %bitcast.3), custom_call_target="tpu_custom_call" | custom-call | tf_op jit(solution)/shard_map/pair_densities/pallas_call | solution.py:360
  96.5 2.4 %copy.7 = f32[2,512,1280]{2,1,0:T(8,128)} copy(f32[2,512,1280]{2,1,0:T(8,128)S(1)} %get-tuple-element.4) | data formatting | bytes 10485760
  98.8 0.6 copy.8
Async XLA Ops:
  0.6 1.7 %copy-start = (bf16[8,512,320]{1,2,0:T(8,128)(2,1)S(1)}, bf16[8,512,320]{1,2,0:T(8,128)(2,1)}, u32[]{:S(2)}) copy-start(bf16[8,512,320]{1,2,0:T(8,128)(2,1)} %param.3) | copy-start | bytes 7864324
  2.4 0.7 copy-start.1
  3.1 0.7 copy-start.2

commit v3 on v2

--- a/solution.py
+++ b/solution.py
@@ -25,6 +25,7 @@
     held,
     raw,
     relay,
+    back,
     own_t,
     vv,
     amp,
@@ -43,6 +44,8 @@
     recv_sem,
     raw_sem,
     relay_sem,
+    back_send,
+    back_recv,
     vv_send,
     vv_recv,
 ):
@@ -98,17 +101,23 @@
         copy.start()
     pl.semaphore_wait(barrier, len(peers))
 
+    odd = lax.rem(cz, 2)
+    halfway = jnp.where(odd == 1, along_z(2), along_z(3))
+
+    def send_back(side, src, n):
+        send(side, src, back.at[odd, n], back_recv.at[odd, n], (halfway, q))
+
     @pl.when(h == 0)
     def _():
         for d in (1, 2, 3):
             to_slot(0, mine(near[d], 0), X, 0, q, (b, near[d]))
         to_slot(0, mine(near[1], 1), X, 1, q, (b, near[1]))
         to_slot(0, mine(q, 0), Y, 0, q, (ahead, q))
+        send_back(0, mine(q, 1), 0)
         for d in (2, 3):
             to_slot(0, mine(near[d], 0), Y, 0, q, (across, near[d]))
         for d in (2, 3):
             to_slot(0, mine(near[d], 1), X, 1, q, (b, near[d]))
-        to_slot(0, mine(q, 1), Y, 1, q, (ahead, q))
         for d in (2, 3):
             to_slot(0, mine(near[d], 1), Y, 1, q, (across, near[d]))
         for j in range(2):
@@ -117,14 +126,17 @@
 
     @pl.when(h == 1)
     def _():
-        send(1, mine(near[3], 1), relay.at[0], relay_sem.at[0], (across, near[3]))
+        for d in (2, 3):
+            send(1, mine(near[d], 1), relay.at[d - 2], relay_sem.at[d - 2], (across, near[d]))
         for d in (1, 2, 3):
             to_slot(1, mine(near[d], 0), X, 0, q, (b, near[d]))
         to_slot(1, mine(near[1], 1), X, 1, q, (b, near[1]))
-        for j in range(2):
-            to_slot(1, mine(q, j), Z, j, q, (ahead, q))
-            for d in (1, 2, 3)[: 3 - j]:
-                send(1, mine(near[d], j), raw.at[j, d - 1], raw_sem.at[j, d - 1], (ahead, q))
+        to_slot(1, mine(q, 0), Z, 0, q, (ahead, q))
+        send_back(1, mine(near[1], 0), 0)
+        for d in (2, 3):
+            send(1, mine(near[d], 0), raw.at[0, d - 1], raw_sem.at[0, d - 1], (ahead, q))
+        to_slot(1, mine(q, 1), Z, 1, q, (ahead, q))
+        send_back(1, mine(near[1], 1), 1)
 
     acc[...] = jnp.zeros_like(acc)
     vv[...] = jnp.zeros_like(vv)
@@ -135,40 +147,70 @@
 
         @pl.when(h == 0)
         def _():
-            to_slot(0, slot(X, j, near[d]), Y, j, near[d], (ahead, q))
+            if (j, d) == (1, 1):
+                send_back(0, slot(X, j, near[d]), 1)
+            else:
+                to_slot(0, slot(X, j, near[d]), Y, j, near[d], (ahead, q))
+
+        if d > 1:
+
+            @pl.when(h == 1)
+            def _():
+                to_slot(1, slot(X, j, near[d]), Z, j, near[d], (ahead, q))
 
     def passed_on(j, d):
         @pl.when(h == 1)
         def _():
             if d == 0:
                 slot_arrived(Z, j, q)
-                if j == 1:
-                    send(1, slot(Z, j, q), relay.at[1], relay_sem.at[1], (across, near[2]))
-                    return
                 to_slot(1, slot(Z, j, q), Z, j, q, (across, q))
-                for own in (2, 3):
-                    to_slot(1, mine(near[own], 1), X, 1, q, (b, near[own]))
+                if j == 0:
+                    for own in (2, 3):
+                        to_slot(1, mine(near[own], 1), X, 1, q, (b, near[own]))
                 return
             src = raw.at[j, d - 1]
             arrived(src, raw_sem.at[j, d - 1])
             to_slot(1, src, Z, j, q, (across, near[d]))
-            if d == 1 or j == 0:
+            if d == 1:
                 to_slot(1, src, Z, j, q, (b, near[d]))
 
-    def second_way():
-        @pl.when(h == 1)
+    def relayed():
+        @pl.when(h == 0)
         def _():
             for d in (2, 3):
-                to_slot(1, slot(X, 1, near[d]), Z, 1, near[d], (ahead, q))
-
-    def relayed(n):
-        @pl.when(h == 0)
-        def _():
-            arrived(relay.at[n], relay_sem.at[n])
-            if n == 0:
-                to_slot(0, relay.at[n], Z, 1, near[3], (ahead, q))
-            else:
-                to_slot(0, relay.at[n], Z, 1, near[2], (b, near[2]))
+                arrived(relay.at[d - 2], relay_sem.at[d - 2])
+                to_slot(0, relay.at[d - 2], Z, 1, near[d], (ahead, q))
+
+    def handed_back(n, act):
+        for e in (0, 1):
+            source = cx * RING + lax.rem(cz + 1 + e, RING)
+            device = (lax.rem(2 * source + 2 + h, blocks), q)
+            copy = functools.partial(
+                pltpu.make_async_remote_copy,
+                src_ref=back.at[e, n], send_sem=back_send.at[e, n], device_id=device, device_id_type=MESH,
+            )
+            to_raw = copy(dst_ref=raw.at[n, 0], recv_sem=raw_sem.at[n, 0])
+            if act == "wait":
+
+                @pl.when(odd == 1)
+                def _():
+                    to_raw.wait_send()
+
+                continue
+
+            @pl.when(odd == 1)
+            def _():
+                arrived(back.at[e, n], back_recv.at[e, n])
+
+            @pl.when(jnp.logical_and(odd == 1, h == 1))
+            def _():
+                to_raw.start()
+
+            p = near[n]
+
+            @pl.when(jnp.logical_and(odd == 1, h == 0))
+            def _():
+                copy(dst_ref=slot(Y, 1, p), recv_sem=recv_sem.at[Y, 1, p]).start()
 
     def last_piece(j):
         @pl.when(h == 0)
@@ -186,25 +228,30 @@
     def before(t):
         @pl.when(t == 1)
         def _():
-            passed_on(0, 2)
+            passed_on(0, 3)
+            handed_back(0, "start")
             own_piece(1, 2)
-            passed_on(0, 3)
+            passed_on(1, 0)
             own_piece(1, 3)
-            second_way()
-            relayed(0)
-            passed_on(1, 0)
+            relayed()
             turned(1)
 
+        @pl.when(t == 2)
+        def _():
+            handed_back(1, "start")
+
+        @pl.when(t == 3)
+        def _():
+            passed_on(0, 1)
+
         @pl.when(t == 4)
         def _():
-            passed_on(1, 1)
-            relayed(1)
             for p in range(4):
                 slot_arrived(Y, 0, p)
 
         @pl.when(t == 6)
         def _():
-            passed_on(1, 2)
+            passed_on(1, 1)
             last_piece(0)
 
         @pl.when(t == 8)
@@ -223,12 +270,12 @@
     own_piece(0, 2)
     passed_on(0, 0)
     own_piece(0, 3)
-    passed_on(0, 1)
+    passed_on(0, 2)
     turned(0)
 
     size = vir_ref.shape[1]
 
-    pairs = 4 * CYCLE
+    pairs, late = 4 * CYCLE, tilde.shape[0]
 
     def place(t):
         turn = t // 2
@@ -241,13 +288,13 @@
         other = held.at[which * 2 + j]
         for n in range(held.shape[1] // 256):
             rows = pl.ds(n * 256, 256)
-            acc[i, :, rows] += lax.dot_general(tilde[i], other[rows, :], NT, preferred_element_type=jnp.float32)
+            acc[i, :, rows] += lax.dot_general(tilde[lax.rem(t, late)], other[rows, :], NT, preferred_element_type=jnp.float32)
 
     def pair(t, carry):
         before(t)
         i, which, j = place(t)
-        back = jnp.where(which == X, 0, jnp.where(which == Y, 2 - h, 1 + h))
-        partner = lax.rem(b - back + blocks, blocks)
+        behind_by = jnp.where(which == X, 0, jnp.where(which == Y, 2 - h, 1 + h))
+        partner = lax.rem(b - behind_by + blocks, blocks)
         e_i = occ_ref[(b * 4 + q) * 2 + i]
         e_j = occ_ref[(partner * 4 + q) * 2 + j]
         other = held.at[which * 2 + j]
@@ -262,10 +309,10 @@
                 amp_b[:, lanes] = ratio.astype(jnp.bfloat16)
         for n in range(size // 128):
             rows = pl.ds(n * 128, 128)
-            tilde[i, rows, :] = (2.0 * amp[rows, :] - jnp.transpose(amp[:, rows])).astype(jnp.bfloat16)
-        vv[...] += lax.dot_general(amp_b[...], tilde[i], NT, preferred_element_type=jnp.float32)
-
-        @pl.when(t < pairs - 2)
+            tilde[lax.rem(t, late), rows, :] = (2.0 * amp[rows, :] - jnp.transpose(amp[:, rows])).astype(jnp.bfloat16)
+        vv[...] += lax.dot_general(amp_b[...], tilde[lax.rem(t, late)], NT, preferred_element_type=jnp.float32)
+
+        @pl.when(t < pairs - late)
         def _():
             to_gamma(t)
 
@@ -288,8 +335,8 @@
         device_id=(b, near[1]), device_id_type=MESH,
     )
     swap.start()
-    to_gamma(pairs - 2)
-    to_gamma(pairs - 1)
+    to_gamma(pairs - 4)
+    to_gamma(pairs - 3)
     swap.wait()
     half_in[...] += halves[k]
 
@@ -326,6 +373,8 @@
 
     orders = ("yzx", "xzy")
     waits = [stage(half_in.at[n].reshape(RING, square, 8, 128), first_in.at[n], 1 + 3 * n, orders[n][0]) for n in range(2)]
+    to_gamma(pairs - 2)
+    to_gamma(pairs - 1)
     for n in range(2):
         second[n] = waits[n]()
         waits[n] = stage(second.at[n].reshape(RING, RING, 8, 128), second_in.at[n], 7 + 3 * n, orders[n][1])
@@ -338,6 +387,8 @@
         vv_ref[:, lanes] = total[0:4]
         vv_ref[:, pl.ds(256 + n * 128, 128)] = total[4:8]
 
+    for n in range(2):
+        handed_back(n, "wait")
     for side in (0, 1):
 
         @pl.when(h == side)
@@ -373,11 +424,12 @@
             pltpu.VMEM((3 * pair_rows, naux, size), bf16),
             pltpu.VMEM((pair_rows, 3, piece, size), bf16),
             pltpu.VMEM((2, piece, size), bf16),
+            pltpu.VMEM((2, 2, piece, size), bf16),
             pltpu.VMEM((pair_rows, size, naux), bf16),
             pltpu.VMEM((size, size), f32),
             pltpu.VMEM((size, size), f32),
             pltpu.VMEM((size, size), bf16),
-            pltpu.VMEM((pair_rows, size, size), bf16),
+            pltpu.VMEM((4, size, size), bf16),
             pltpu.VMEM((size, 128), f32),
             pltpu.VMEM((2, 2, chips, 8, 128), f32),
             pltpu.VMEM((2, chips, 8, 128), f32),
@@ -391,6 +443,8 @@
             dma((3, 2, 4)),
             dma((2, 3)),
             dma((2,)),
+            dma((2, 2)),
+            dma((2, 2)),
             dma((19,)),
             dma((19,)),
         ],
@@ -398,7 +452,7 @@
             collective_id=0, has_side_effects=True, vmem_limit_bytes=40 * 2**20
         ),
         name="pair_densities",
-    )(jnp.swapaxes(bints, 1, 2), occ_energy, vir_energy.reshape(1, size))
+    )(pltpu.with_memory_space_constraint(jnp.swapaxes(bints, 1, 2), pltpu.HBM), pltpu.with_memory_space_constraint(occ_energy, pltpu.HBM), pltpu.with_memory_space_constraint(vir_energy.reshape(1, size), pltpu.HBM))
 
 
 def solution(mesh):

time: 101 us -> 94.9 us (0.940)
  local copies, waits for them, and re-layouts: 6.05 us -> 2.96 us
  Pallas kernels: 92.7 us -> 90 us
    unnamed x8 -> x2, local copies, waits for them, and re-layouts: 6.05 us -> 2.96 us
    pallas_call x1, Pallas kernels: 92.7 us -> 90 us  [per_device(): pl.pallas_call(functools.partial(kernel, blocks, scale), out_shape=(jax.S...]
where the time goes in v3:
time: 94.9 us; the launch traced here: 93.5 us
  Pallas kernels  90 us (95%)
  local copies, waits for them, and re-layouts  2.96 us (3%)
    pallas_call x1, Pallas kernels, per_device(): pl.pallas_call(functools.partial(kernel, blocks, scale), out_shape=(jax.S...  90 us
    unnamed x2, local copies, waits for them, and re-layouts  2.96 us

profile of v3, /device:TPU:1, one launch (start us, length us, event | category | flops | bytes accessed | tf_op | source)
XLA Modules:
  0.0 93.5 jit_solution(14603410828765231997)
XLA Ops:
  0.6 90.0 %pair_densities.1 = (f32[2,512,1280]{2,1,0:T(8,128)S(1)}, f32[4,512]{1,0:T(4,128)S(1)}) custom-call(bf16[8,320,512]{2,1,0:T(8,128)(2,1)} %bitcast.2, f32[256]{0:T(256)} %occ_ref.1, f32[1,512]{1,0:T(1,128)} %bitcast.3), custom_call_target="tpu_custom_call" | custom-call | tf_op jit(solution)/shard_map/pair_densities/pallas_call | solution.py:411
  90.6 2.4 %copy.7 = f32[2,512,1280]{2,1,0:T(8,128)} copy(f32[2,512,1280]{2,1,0:T(8,128)S(1)} %get-tuple-element.4) | data formatting | bytes 10485760
  92.9 0.6 copy.8

commit v4 on v3

--- a/solution.py
+++ b/solution.py
@@ -232,14 +232,11 @@
             handed_back(0, "start")
             own_piece(1, 2)
             passed_on(1, 0)
+            handed_back(1, "start")
             own_piece(1, 3)
             relayed()
             turned(1)
 
-        @pl.when(t == 2)
-        def _():
-            handed_back(1, "start")
-
         @pl.when(t == 3)
         def _():
             passed_on(0, 1)
@@ -249,9 +246,12 @@
             for p in range(4):
                 slot_arrived(Y, 0, p)
 
+        @pl.when(t == 5)
+        def _():
+            passed_on(1, 1)
+
         @pl.when(t == 6)
         def _():
-            passed_on(1, 1)
             last_piece(0)
 
         @pl.when(t == 8)

time: 94.9 us -> 93.4 us (0.984)
  Pallas kernels: 90 us -> 88.8 us
    pallas_call x1, Pallas kernels: 90 us -> 88.8 us  [per_device(): pl.pallas_call(functools.partial(kernel, blocks, scale), out_shape=(jax.S...]
where the time goes in v4:
time: 93.4 us; the launch traced here: 92.4 us
  Pallas kernels  88.8 us (95%)
  local copies, waits for them, and re-layouts  2.96 us (3%)
    pallas_call x1, Pallas kernels, per_device(): pl.pallas_call(functools.partial(kernel, blocks, scale), out_shape=(jax.S...  88.8 us
    unnamed x2, local copies, waits for them, and re-layouts  2.96 us

profile of v4, /device:TPU:1, one launch (start us, length us, event | category | flops | bytes accessed | tf_op | source)
XLA Modules:
  0.0 92.4 jit_solution(16684229874164511617)
XLA Ops:
  0.6 88.8 %pair_densities.1 = (f32[2,512,1280]{2,1,0:T(8,128)S(1)}, f32[4,512]{1,0:T(4,128)S(1)}) custom-call(bf16[8,320,512]{2,1,0:T(8,128)(2,1)} %bitcast.2, f32[256]{0:T(256)} %occ_ref.1, f32[1,512]{1,0:T(1,128)} %bitcast.3), custom_call_target="tpu_custom_call" | custom-call | tf_op jit(solution)/shard_map/pair_densities/pallas_call | solution.py:411
  89.4 2.4 %copy.7 = f32[2,512,1280]{2,1,0:T(8,128)} copy(f32[2,512,1280]{2,1,0:T(8,128)S(1)} %get-tuple-element.4) | data formatting | bytes 10485760
  91.8 0.6 copy.8

commit v5 on v4

--- a/solution.py
+++ b/solution.py
@@ -34,11 +34,7 @@
     vir_col,
     halves,
     half_in,
-    first_in,
-    second,
-    second_in,
-    third,
-    third_in,
+    parts,
     local_sem,
     send_sem,
     recv_sem,
@@ -48,6 +44,7 @@
     back_recv,
     vv_send,
     vv_recv,
+    known,
 ):
     piece = x_ref.shape[1]
     b, q = lax.axis_index("blk"), lax.axis_index("quarter")
@@ -138,6 +135,8 @@
         to_slot(1, mine(q, 1), Z, 1, q, (ahead, q))
         send_back(1, mine(near[1], 1), 1)
 
+    for s in (1, 2, 3):
+        pl.semaphore_signal(known.at[0], inc=1, device_id=(along_z(s), q), device_id_type=MESH)
     acc[...] = jnp.zeros_like(acc)
     vv[...] = jnp.zeros_like(vv)
     vir_col[...] = jnp.transpose(jnp.broadcast_to(vir_ref[...], (128, vir_ref.shape[1])))
@@ -271,6 +270,9 @@
     passed_on(0, 0)
     own_piece(0, 3)
     passed_on(0, 2)
+    pl.semaphore_wait(known.at[0], 3)
+    for s in (1, 2, 3):
+        pl.semaphore_signal(known.at[1], inc=1, device_id=(along_x(s), q), device_id_type=MESH)
     turned(0)
 
     size = vir_ref.shape[1]
@@ -321,71 +323,45 @@
     lax.fori_loop(0, pairs, pair, 0)
 
     low = lax.broadcasted_iota(jnp.int32, (8, 256), 0) < 4
-    square = RING * RING
     for chip in range(size // 8):
-        spot = (chip % RING) * square + ((chip // RING) % RING) * RING + chip // square
         rows = pl.ds(chip * 8, 8)
         left, right = vv[rows, 0:256], vv[rows, 256:512]
-        for core, block in enumerate((jnp.where(low, left, pltpu.roll(right, 4, 0)), jnp.where(low, pltpu.roll(left, 4, 0), right))):
-            halves[core, 0, spot] = block[:, 0:128]
-            halves[core, 1, chip] = block[:, 128:256]
+        halves[0, chip] = jnp.where(low, left, pltpu.roll(right, 4, 0))
+        halves[1, chip] = jnp.where(low, pltpu.roll(left, 4, 0), right)
 
     swap = pltpu.make_async_remote_copy(
         src_ref=halves.at[1 - k], dst_ref=half_in, send_sem=vv_send.at[0], recv_sem=vv_recv.at[0],
         device_id=(b, near[1]), device_id_type=MESH,
     )
     swap.start()
-    to_gamma(pairs - 4)
-    to_gamma(pairs - 3)
+    to_gamma(pairs - 6)
+    to_gamma(pairs - 5)
+    pl.semaphore_wait(known.at[1], 3)
     swap.wait()
     half_in[...] += halves[k]
 
     here = 2 * h + l
-    column = []
-    for s in (1, 2, 3):
-        there = lax.rem(here + s, RING)
-        column.append((2 * col + there // 2, 2 * lax.rem(there, 2) + k))
-    rings = {
-        "y": (here, column),
-        "z": (cz, [(along_z(s), q) for s in (1, 2, 3)]),
-        "x": (cx, [(along_x(s), q) for s in (1, 2, 3)]),
-    }
-
-    def stage(src, landing, first, axis):
-        me, devices = rings[axis]
-        copies = [
-            pltpu.make_async_remote_copy(
-                src_ref=src.at[lax.rem(me + s, RING)], dst_ref=landing.at[s - 1],
-                send_sem=vv_send.at[first + s - 1], recv_sem=vv_recv.at[first + s - 1],
-                device_id=devices[s - 1], device_id_type=MESH,
-            )
-            for s in (1, 2, 3)
-        ]
-        for copy in copies:
-            copy.start()
-
-        def total():
-            for copy in copies:
-                copy.wait()
-            return src[me] + landing[0] + landing[1] + landing[2]
-
-        return total
-
-    orders = ("yzx", "xzy")
-    waits = [stage(half_in.at[n].reshape(RING, square, 8, 128), first_in.at[n], 1 + 3 * n, orders[n][0]) for n in range(2)]
-    to_gamma(pairs - 2)
-    to_gamma(pairs - 1)
-    for n in range(2):
-        second[n] = waits[n]()
-        waits[n] = stage(second.at[n].reshape(RING, RING, 8, 128), second_in.at[n], 7 + 3 * n, orders[n][1])
-    for n in range(2):
-        third[n] = waits[n]()
-        waits[n] = stage(third.at[n], third_in.at[n], 13 + 3 * n, orders[n][2])
-    for n in range(2):
-        total = waits[n]() * scale
-        lanes = pl.ds(n * 128, 128)
-        vv_ref[:, lanes] = total[0:4]
-        vv_ref[:, pl.ds(256 + n * 128, 128)] = total[4:8]
+    offsets = [(dx, dz, dy) for dx in range(RING) for dz in range(RING) for dy in range(RING) if dx or dz or dy]
+    offsets.sort(key=lambda o: -sum(min(d, RING - d) for d in o))
+    turns = {d: (lax.rem(cx + d, RING), lax.rem(cz + d, RING), lax.rem(here + d, RING)) for d in range(RING)}
+    for n, (dx, dz, dy) in enumerate(offsets):
+        tx, tz, ty = turns[dx][0], turns[dz][1], turns[dy][2]
+        column = tx * RING + tz
+        pltpu.make_async_remote_copy(
+            src_ref=half_in.at[column * RING + ty], dst_ref=parts.at[n], send_sem=vv_send.at[1], recv_sem=vv_recv.at[1],
+            device_id=(2 * column + ty // 2, 2 * lax.rem(ty, 2) + k), device_id_type=MESH,
+        ).start()
+    for n in (4, 3, 2, 1):
+        to_gamma(pairs - n)
+    everything = pltpu.make_async_remote_copy(
+        src_ref=parts, dst_ref=parts, send_sem=vv_send.at[1], recv_sem=vv_recv.at[1],
+        device_id=(b, near[1]), device_id_type=MESH,
+    )
+    everything.wait_recv()
+    total = (half_in[(cx * RING + cz) * RING + here] + jnp.sum(parts[...], axis=0)) * scale
+    vv_ref[:, 0:256] = total[0:4]
+    vv_ref[:, 256:512] = total[4:8]
+    everything.wait_send()
 
     for n in range(2):
         handed_back(n, "wait")
@@ -429,15 +405,11 @@
             pltpu.VMEM((size, size), f32),
             pltpu.VMEM((size, size), f32),
             pltpu.VMEM((size, size), bf16),
-            pltpu.VMEM((4, size, size), bf16),
+            pltpu.VMEM((6, size, size), bf16),
             pltpu.VMEM((size, 128), f32),
-            pltpu.VMEM((2, 2, chips, 8, 128), f32),
-            pltpu.VMEM((2, chips, 8, 128), f32),
-            pltpu.VMEM((2, 3, 16, 8, 128), f32),
-            pltpu.VMEM((2, 16, 8, 128), f32),
-            pltpu.VMEM((2, 3, 4, 8, 128), f32),
-            pltpu.VMEM((2, 4, 8, 128), f32),
-            pltpu.VMEM((2, 3, 8, 128), f32),
+            pltpu.VMEM((2, chips, 8, 256), f32),
+            pltpu.VMEM((chips, 8, 256), f32),
+            pltpu.VMEM((chips - 1, 8, 256), f32),
             dma((2,)),
             dma((40,)),
             dma((3, 2, 4)),
@@ -445,8 +417,9 @@
             dma((2,)),
             dma((2, 2)),
             dma((2, 2)),
-            dma((19,)),
-            dma((19,)),
+            dma((2,)),
+            dma((2,)),
+            pltpu.SemaphoreType.REGULAR((2,)),
         ],
         compiler_params=pltpu.CompilerParams(
             collective_id=0, has_side_effects=True, vmem_limit_bytes=40 * 2**20

time: 93.4 us -> 88.8 us (0.951)
  Pallas kernels: 88.8 us -> 85 us
    pallas_call x1, Pallas kernels: 88.8 us -> 85 us  [per_device(): pl.pallas_call(functools.partial(kernel, blocks, scale), out_shape=(jax.S...]
where the time goes in v5:
time: 88.8 us; the launch traced here: 88.6 us
  Pallas kernels  85 us (96%)
  local copies, waits for them, and re-layouts  2.96 us (3%)
    pallas_call x1, Pallas kernels, per_device(): pl.pallas_call(functools.partial(kernel, blocks, scale), out_shape=(jax.S...  85 us
    unnamed x2, local copies, waits for them, and re-layouts  2.96 us

profile of v5, /device:TPU:1, one launch (start us, length us, event | category | flops | bytes accessed | tf_op | source)
XLA Modules:
  0.0 88.6 jit_solution(8454186922441616775)
XLA Ops:
  0.6 85.0 %pair_densities.1 = (f32[2,512,1280]{2,1,0:T(8,128)S(1)}, f32[4,512]{1,0:T(4,128)S(1)}) custom-call(bf16[8,320,512]{2,1,0:T(8,128)(2,1)} %bitcast.2, f32[256]{0:T(256)} %occ_ref.1, f32[1,512]{1,0:T(1,128)} %bitcast.3), custom_call_target="tpu_custom_call" | custom-call | tf_op jit(solution)/shard_map/pair_densities/pallas_call | solution.py:387
  85.7 2.4 %copy.7 = f32[2,512,1280]{2,1,0:T(8,128)} copy(f32[2,512,1280]{2,1,0:T(8,128)S(1)} %get-tuple-element.4) | data formatting | bytes 10485760
  88.0 0.6 copy.8

commit v6 on v5

--- a/solution.py
+++ b/solution.py
@@ -141,17 +141,19 @@
     vv[...] = jnp.zeros_like(vv)
     vir_col[...] = jnp.transpose(jnp.broadcast_to(vir_ref[...], (128, vir_ref.shape[1])))
 
-    def own_piece(j, d):
+    def own_piece(j, d, sides=(0, 1)):
         slot_arrived(X, j, near[d])
 
-        @pl.when(h == 0)
-        def _():
-            if (j, d) == (1, 1):
-                send_back(0, slot(X, j, near[d]), 1)
-            else:
-                to_slot(0, slot(X, j, near[d]), Y, j, near[d], (ahead, q))
-
-        if d > 1:
+        if 0 in sides:
+
+            @pl.when(h == 0)
+            def _():
+                if (j, d) == (1, 1):
+                    send_back(0, slot(X, j, near[d]), 1)
+                else:
+                    to_slot(0, slot(X, j, near[d]), Y, j, near[d], (ahead, q))
+
+        if d > 1 and 1 in sides:
 
             @pl.when(h == 1)
             def _():
@@ -224,41 +226,27 @@
             rows = pl.ds(n * 256, 256)
             own_t[i, :, rows] = jnp.transpose(held[2 * X + i, rows, :])
 
-    def before(t):
-        @pl.when(t == 1)
-        def _():
-            passed_on(0, 3)
-            handed_back(0, "start")
-            own_piece(1, 2)
-            passed_on(1, 0)
-            handed_back(1, "start")
-            own_piece(1, 3)
-            relayed()
-            turned(1)
-
-        @pl.when(t == 3)
+    def before(turn):
+        @pl.when(turn == 1)
         def _():
             passed_on(0, 1)
 
-        @pl.when(t == 4)
+        @pl.when(turn == 2)
         def _():
             for p in range(4):
                 slot_arrived(Y, 0, p)
 
-        @pl.when(t == 5)
+        @pl.when(turn == 3)
         def _():
             passed_on(1, 1)
-
-        @pl.when(t == 6)
-        def _():
             last_piece(0)
 
-        @pl.when(t == 8)
+        @pl.when(turn == 4)
         def _():
             for p in range(4):
                 slot_arrived(Y, 1, p)
 
-        @pl.when(t == 10)
+        @pl.when(turn == 5)
         def _():
             last_piece(1)
 
@@ -274,53 +262,85 @@
     for s in (1, 2, 3):
         pl.semaphore_signal(known.at[1], inc=1, device_id=(along_x(s), q), device_id_type=MESH)
     turned(0)
+    passed_on(0, 3)
+
+    @pl.when(h == 0)
+    def _():
+        own_piece(1, 2, (0,))
+        handed_back(0, "start")
+        own_piece(1, 3, (0,))
+
+    relayed()
+
+    @pl.when(h == 0)
+    def _():
+        handed_back(1, "start")
+
+    @pl.when(h == 1)
+    def _():
+        handed_back(0, "start")
+        own_piece(1, 2, (1,))
+
+    passed_on(1, 0)
+
+    @pl.when(h == 1)
+    def _():
+        handed_back(1, "start")
+        own_piece(1, 3, (1,))
+
+    turned(1)
 
     size = vir_ref.shape[1]
 
-    pairs, late = 4 * CYCLE, tilde.shape[0]
-
-    def place(t):
-        turn = t // 2
+    turns, late = 2 * CYCLE, tilde.shape[0]
+    rows_both = 2 * size
+
+    def place(turn):
         which = jnp.where(turn < 2, X, Y + lax.rem(turn, 2))
-        j = jnp.where(turn < 2, turn, (turn - 2) // 2)
-        return lax.rem(t, 2), which, j
-
-    def to_gamma(t):
-        i, which, j = place(t)
+        return which, jnp.where(turn < 2, turn, (turn - 2) // 2)
+
+    def to_gamma(turn):
+        which, j = place(turn)
         other = held.at[which * 2 + j]
+        both = tilde[lax.rem(turn, late)].reshape(rows_both, size)
         for n in range(held.shape[1] // 256):
             rows = pl.ds(n * 256, 256)
-            acc[i, :, rows] += lax.dot_general(tilde[lax.rem(t, late)], other[rows, :], NT, preferred_element_type=jnp.float32)
-
-    def pair(t, carry):
-        before(t)
-        i, which, j = place(t)
+            terms = lax.dot_general(both, other[rows, :], NT, preferred_element_type=jnp.float32)
+            acc[:, :, rows] += terms.reshape(2, size, 256)
+
+    def pairs(turn, carry):
+        before(turn)
+        which, j = place(turn)
+        slot_out = lax.rem(turn, late)
         behind_by = jnp.where(which == X, 0, jnp.where(which == Y, 2 - h, 1 + h))
         partner = lax.rem(b - behind_by + blocks, blocks)
-        e_i = occ_ref[(b * 4 + q) * 2 + i]
         e_j = occ_ref[(partner * 4 + q) * 2 + j]
         other = held.at[which * 2 + j]
         for n in range(size // 256):
             cols = pl.ds(n * 256, 256)
-            pairint = jnp.dot(own_t[i], other[:, cols], preferred_element_type=jnp.float32)
-            for m in range(2):
-                lanes = pl.ds(n * 256 + m * 128, 128)
-                denom = vir_col[...] + vir_ref[:, lanes] - e_i - e_j
-                ratio = pairint[:, m * 128 : (m + 1) * 128] / denom
-                amp[:, lanes] = ratio
-                amp_b[:, lanes] = ratio.astype(jnp.bfloat16)
-        for n in range(size // 128):
-            rows = pl.ds(n * 128, 128)
-            tilde[lax.rem(t, late), rows, :] = (2.0 * amp[rows, :] - jnp.transpose(amp[:, rows])).astype(jnp.bfloat16)
-        vv[...] += lax.dot_general(amp_b[...], tilde[lax.rem(t, late)], NT, preferred_element_type=jnp.float32)
-
-        @pl.when(t < pairs - late)
-        def _():
-            to_gamma(t)
+            pairint = jnp.dot(own_t[...].reshape(rows_both, -1), other[:, cols], preferred_element_type=jnp.float32)
+            for i in range(2):
+                e_i = occ_ref[(b * 4 + q) * 2 + i]
+                for m in range(2):
+                    lanes = pl.ds(n * 256 + m * 128, 128)
+                    denom = vir_col[...] + vir_ref[:, lanes] - e_i - e_j
+                    ratio = pairint[i * size : (i + 1) * size, m * 128 : (m + 1) * 128] / denom
+                    amp[i, :, lanes] = ratio
+                    amp_b[i, :, lanes] = ratio.astype(jnp.bfloat16)
+        for i in range(2):
+            for n in range(size // 128):
+                rows = pl.ds(n * 128, 128)
+                turned_back = jnp.transpose(amp[i, :, rows])
+                tilde[slot_out, i, rows, :] = (2.0 * amp[i, rows, :] - turned_back).astype(jnp.bfloat16)
+            vv[...] += lax.dot_general(amp_b[i], tilde[slot_out, i], NT, preferred_element_type=jnp.float32)
+
+        @pl.when(turn < turns - late)
+        def _():
+            to_gamma(turn)
 
         return carry
 
-    lax.fori_loop(0, pairs, pair, 0)
+    lax.fori_loop(0, turns, pairs, 0)
 
     low = lax.broadcasted_iota(jnp.int32, (8, 256), 0) < 4
     for chip in range(size // 8):
@@ -334,8 +354,6 @@
         device_id=(b, near[1]), device_id_type=MESH,
     )
     swap.start()
-    to_gamma(pairs - 6)
-    to_gamma(pairs - 5)
     pl.semaphore_wait(known.at[1], 3)
     swap.wait()
     half_in[...] += halves[k]
@@ -343,16 +361,16 @@
     here = 2 * h + l
     offsets = [(dx, dz, dy) for dx in range(RING) for dz in range(RING) for dy in range(RING) if dx or dz or dy]
     offsets.sort(key=lambda o: -sum(min(d, RING - d) for d in o))
-    turns = {d: (lax.rem(cx + d, RING), lax.rem(cz + d, RING), lax.rem(here + d, RING)) for d in range(RING)}
+    moved = {d: (lax.rem(cx + d, RING), lax.rem(cz + d, RING), lax.rem(here + d, RING)) for d in range(RING)}
     for n, (dx, dz, dy) in enumerate(offsets):
-        tx, tz, ty = turns[dx][0], turns[dz][1], turns[dy][2]
+        tx, tz, ty = moved[dx][0], moved[dz][1], moved[dy][2]
         column = tx * RING + tz
         pltpu.make_async_remote_copy(
             src_ref=half_in.at[column * RING + ty], dst_ref=parts.at[n], send_sem=vv_send.at[1], recv_sem=vv_recv.at[1],
             device_id=(2 * column + ty // 2, 2 * lax.rem(ty, 2) + k), device_id_type=MESH,
         ).start()
-    for n in (4, 3, 2, 1):
-        to_gamma(pairs - n)
+    for n in (3, 2, 1):
+        to_gamma(turns - n)
     everything = pltpu.make_async_remote_copy(
         src_ref=parts, dst_ref=parts, send_sem=vv_send.at[1], recv_sem=vv_recv.at[1],
         device_id=(b, near[1]), device_id_type=MESH,
@@ -403,9 +421,9 @@
             pltpu.VMEM((2, 2, piece, size), bf16),
             pltpu.VMEM((pair_rows, size, naux), bf16),
             pltpu.VMEM((size, size), f32),
-            pltpu.VMEM((size, size), f32),
-            pltpu.VMEM((size, size), bf16),
-            pltpu.VMEM((6, size, size), bf16),
+            pltpu.VMEM((pair_rows, size, size), f32),
+            pltpu.VMEM((pair_rows, size, size), bf16),
+            pltpu.VMEM((3, pair_rows, size, size), bf16),
             pltpu.VMEM((size, 128), f32),
             pltpu.VMEM((2, chips, 8, 256), f32),
             pltpu.VMEM((chips, 8, 256), f32),

time: 88.8 us -> 88.1 us (level)
  no operation moved by 1% of the time
where the time goes in v6:
time: 88.1 us; the launch traced here: 88 us
  Pallas kernels  84.4 us (96%)
  local copies, waits for them, and re-layouts  2.96 us (3%)
    pallas_call x1, Pallas kernels, per_device(): pl.pallas_call(functools.partial(kernel, blocks, scale), out_shape=(jax.S...  84.4 us
    unnamed x2, local copies, waits for them, and re-layouts  2.96 us

profile of v6, /device:TPU:1, one launch (start us, length us, event | category | flops | bytes accessed | tf_op | source)
XLA Modules:
  0.0 88.0 jit_solution(4821648631937328949)
XLA Ops:
  0.6 84.4 %pair_densities.1 = (f32[2,512,1280]{2,1,0:T(8,128)S(1)}, f32[4,512]{1,0:T(4,128)S(1)}) custom-call(bf16[8,320,512]{2,1,0:T(8,128)(2,1)} %bitcast.2, f32[256]{0:T(256)} %occ_ref.1, f32[1,512]{1,0:T(1,128)} %bitcast.3), custom_call_target="tpu_custom_call" | custom-call | tf_op jit(solution)/shard_map/pair_densities/pallas_call | solution.py:405
  85.0 2.4 %copy.7 = f32[2,512,1280]{2,1,0:T(8,128)} copy(f32[2,512,1280]{2,1,0:T(8,128)S(1)} %get-tuple-element.4) | data formatting | bytes 10485760
  87.4 0.6 copy.8

commit v7 on v6

--- a/solution.py
+++ b/solution.py
@@ -394,6 +394,19 @@
                 ).wait_send()
 
 
+def put_out(gamma_ref, rows_ref, gamma_out, rows_out, sems):
+    copies = [pltpu.make_async_copy(rows_ref, rows_out, sems.at[0])]
+    cut = gamma_ref.shape[1] // 4
+    for i in range(gamma_ref.shape[0]):
+        for n in range(4):
+            part = pl.ds(n * cut, cut)
+            copies.append(pltpu.make_async_copy(gamma_ref.at[i, part], gamma_out.at[i, part], sems.at[1 + 4 * i + n]))
+    for copy in copies:
+        copy.start()
+    for copy in copies:
+        copy.wait()
+
+
 def per_device(blocks, quarters, bints, occ_energy, vir_energy):
     rows, size, piece = bints.shape
     naux = piece * quarters
@@ -402,7 +415,7 @@
     scale = 1.0 / float(pair_rows * blocks * quarters * CYCLE * pair_rows)
     dma = pltpu.SemaphoreType.DMA
     chips = size // 8
-    return pl.pallas_call(
+    gamma, rows_own = pl.pallas_call(
         functools.partial(kernel, blocks, scale),
         out_shape=(
             jax.ShapeDtypeStruct((pair_rows, size, naux), f32),
@@ -445,6 +458,16 @@
         name="pair_densities",
     )(pltpu.with_memory_space_constraint(jnp.swapaxes(bints, 1, 2), pltpu.HBM), pltpu.with_memory_space_constraint(occ_energy, pltpu.HBM), pltpu.with_memory_space_constraint(vir_energy.reshape(1, size), pltpu.HBM))
 
+    return pl.pallas_call(
+        put_out,
+        out_shape=(jax.ShapeDtypeStruct(gamma.shape, f32), jax.ShapeDtypeStruct(rows_own.shape, f32)),
+        in_specs=[pl.BlockSpec(memory_space=pl.ANY)] * 2,
+        out_specs=(pl.BlockSpec(memory_space=pl.ANY),) * 2,
+        scratch_shapes=[dma((1 + 4 * pair_rows,))],
+        compiler_params=pltpu.CompilerParams(vmem_limit_bytes=2**20),
+        name="put_out",
+    )(gamma, rows_own)
+
 
 def solution(mesh):
     return jax.shard_map(

time: 88.1 us -> 87.6 us (level)
  local copies, waits for them, and re-layouts: 2.96 us -> 0 us
  Pallas kernels: 84.4 us -> 86.8 us
    unnamed x2 -> x0, local copies, waits for them, and re-layouts: 2.96 us -> none
    pallas_call x0 -> x1, Pallas kernels: none -> 2.43 us  [per_device(): pl.pallas_call(put_out, out_shape=(jax.ShapeDtypeStruct(gamma.shape, f32)...]
where the time goes in v7:
time: 87.6 us; the launch traced here: 87.5 us
  Pallas kernels  86.8 us (99%)
    pallas_call x1, Pallas kernels, per_device(): pl.pallas_call(functools.partial(kernel, blocks, scale), out_shape=(jax.S...  84.4 us
    pallas_call x1, Pallas kernels, per_device(): pl.pallas_call(put_out, out_shape=(jax.ShapeDtypeStruct(gamma.shape, f32)...  2.43 us

profile of v7, /device:TPU:1, one launch (start us, length us, event | category | flops | bytes accessed | tf_op | source)
XLA Modules:
  0.0 87.5 jit_solution(17833939099473317169)
XLA Ops:
  0.6 84.4 %pair_densities.1 = (f32[2,512,1280]{2,1,0:T(8,128)S(1)}, f32[4,512]{1,0:T(4,128)S(1)}) custom-call(bf16[8,320,512]{2,1,0:T(8,128)(2,1)} %bitcast.2, f32[256]{0:T(256)} %occ_ref.1, f32[1,512]{1,0:T(1,128)} %bitcast.3), custom_call_target="tpu_custom_call" | custom-call | tf_op jit(solution)/shard_map/pair_densities/pallas_call | solution.py:418
  85.0 2.4 %put_out.1 = (f32[2,512,1280]{2,1,0:T(8,128)}, f32[4,512]{1,0:T(4,128)}) custom-call(f32[2,512,1280]{2,1,0:T(8,128)S(1)} %get-tuple-element.4.gamma_ref, f32[4,512]{1,0:T(4,128)S(1)} %get-tuple-element.5.rows_ref), custom_call_target="tpu_custom_call" | custom-call | tf_op jit(solution)/shard_map/put_out/pallas_call | solution.py:461

commit v8 on v7

--- a/solution.py
+++ b/solution.py
@@ -343,20 +343,25 @@
     lax.fori_loop(0, turns, pairs, 0)
 
     low = lax.broadcasted_iota(jnp.int32, (8, 256), 0) < 4
-    for chip in range(size // 8):
-        rows = pl.ds(chip * 8, 8)
-        left, right = vv[rows, 0:256], vv[rows, 256:512]
-        halves[0, chip] = jnp.where(low, left, pltpu.roll(right, 4, 0))
-        halves[1, chip] = jnp.where(low, pltpu.roll(left, 4, 0), right)
-
-    swap = pltpu.make_async_remote_copy(
-        src_ref=halves.at[1 - k], dst_ref=half_in, send_sem=vv_send.at[0], recv_sem=vv_recv.at[0],
-        device_id=(b, near[1]), device_id_type=MESH,
-    )
-    swap.start()
+    swaps = []
+    for half in range(2):
+        part = pl.ds(half * (size // 16), size // 16)
+        for chip in range(half * (size // 16), (half + 1) * (size // 16)):
+            rows = pl.ds(chip * 8, 8)
+            left, right = vv[rows, 0:256], vv[rows, 256:512]
+            halves[0, chip] = jnp.where(low, left, pltpu.roll(right, 4, 0))
+            halves[1, chip] = jnp.where(low, pltpu.roll(left, 4, 0), right)
+        swap = pltpu.make_async_remote_copy(
+            src_ref=halves.at[1 - k, part], dst_ref=half_in.at[part],
+            send_sem=vv_send.at[2 * half], recv_sem=vv_recv.at[2 * half],
+            device_id=(b, near[1]), device_id_type=MESH,
+        )
+        swap.start()
+        swaps.append((swap, part))
     pl.semaphore_wait(known.at[1], 3)
-    swap.wait()
-    half_in[...] += halves[k]
+    for swap, part in swaps:
+        swap.wait()
+        half_in[part] += halves[k, part]
 
     here = 2 * h + l
     offsets = [(dx, dz, dy) for dx in range(RING) for dz in range(RING) for dy in range(RING) if dx or dz or dy]
@@ -448,8 +453,8 @@
             dma((2,)),
             dma((2, 2)),
             dma((2, 2)),
-            dma((2,)),
-            dma((2,)),
+            dma((3,)),
+            dma((3,)),
             pltpu.SemaphoreType.REGULAR((2,)),
         ],
         compiler_params=pltpu.CompilerParams(

time: 87.6 us -> 87.5 us (level)
  no operation moved by 1% of the time
where the time goes in v8:
time: 87.5 us; the launch traced here: 87.4 us
  Pallas kernels  86.8 us (99%)
    pallas_call x1, Pallas kernels, per_device(): pl.pallas_call(functools.partial(kernel, blocks, scale), out_shape=(jax.S...  84.3 us
    pallas_call x1, Pallas kernels, per_device(): pl.pallas_call(put_out, out_shape=(jax.ShapeDtypeStruct(gamma.shape, f32)...  2.43 us

profile of v8, /device:TPU:1, one launch (start us, length us, event | category | flops | bytes accessed | tf_op | source)
XLA Modules:
  0.0 87.4 jit_solution(10314862767620100604)
XLA Ops:
  0.6 84.3 %pair_densities.1 = (f32[2,512,1280]{2,1,0:T(8,128)S(1)}, f32[4,512]{1,0:T(4,128)S(1)}) custom-call(bf16[8,320,512]{2,1,0:T(8,128)(2,1)} %bitcast.2, f32[256]{0:T(256)} %occ_ref.1, f32[1,512]{1,0:T(1,128)} %bitcast.3), custom_call_target="tpu_custom_call" | custom-call | tf_op jit(solution)/shard_map/pair_densities/pallas_call | solution.py:423
  85.0 2.4 %put_out.1 = (f32[2,512,1280]{2,1,0:T(8,128)}, f32[4,512]{1,0:T(4,128)}) custom-call(f32[2,512,1280]{2,1,0:T(8,128)S(1)} %get-tuple-element.4.gamma_ref, f32[4,512]{1,0:T(4,128)S(1)} %get-tuple-element.5.rows_ref), custom_call_target="tpu_custom_call" | custom-call | tf_op jit(solution)/shard_map/put_out/pallas_call | solution.py:466
